TPU v7x, 32 devices: a whole 2x2x4 slice. The times are simulated.
32 devices in a mesh: dp: 16 (over z, y, x), tensor: 2 (over core).
Axes of the slice: x: 2, y: 2, z: 4, core: 2. Of those that a mesh axis runs over, the one named last changes fastest.
Arguments:
- hidden: bfloat16 [128, 4096], P('dp'), may hold values from -20 to 20
- gain: bfloat16 [4096], replicated, may hold values from 0.5 to 1.5
- head: bfloat16 [4096, 4096], P(('dp', 'tensor')), may hold values from -32 to 32
- moment: bfloat16 [4096, 4096], P(('dp', 'tensor')), may hold values from -6 to 6
- second: float32 [4096], P(('dp', 'tensor')), may hold values from 0.5 to 50
- labels: int32 [128], P('dp'), may hold values from 0 to 4095
Outputs:
- grad_hidden: bfloat16 [128, 4096], P('dp')
- grad_gain: float32 [4096], replicated
- head_new: bfloat16 [4096, 4096], P(('dp', 'tensor'))
- moment_new: bfloat16 [4096, 4096], P(('dp', 'tensor'))
- second_new: float32 [4096], P(('dp', 'tensor'))
All inputs are finite; a program needn't handle non-finite values.
Results may differ from a plain program's by a relative error of at most 0.01.
Values may be sent and summed in bfloat16 or wider, within the bound.
A program may use at most 64 MiB of HBM per device.

v0:
```python
import jax
import jax.numpy as jnp
from jax import lax
from jax.sharding import PartitionSpec as P

D = 4096
loss_scale = 16.0
beta_one = 0.9
beta_two = 0.999
adam_eps = 1e-08
step_size = 0.02
norm_eps = 1e-05
bias_one = 1.0 - 0.9**10
bias_two = 1.0 - 0.999**10


def inverse_norm(values_f):
    squares = jnp.sum(values_f * values_f, axis=1)
    return lax.rsqrt(squares / D + norm_eps)


def softmax_grad(logits, targets, vocab_ids):
    local_max = jnp.max(logits, axis=1)
    local_sum = jnp.sum(jnp.exp(logits - local_max[:, None]), axis=1)
    global_max = lax.pmax(local_max, ("dp", "tensor"))
    global_sum = lax.psum(local_sum * jnp.exp(local_max - global_max), ("dp", "tensor"))
    onehot = (targets[:, None] == vocab_ids[None, :]).astype(jnp.float32)
    probability = jnp.exp(logits - global_max[:, None]) / global_sum[:, None]
    return (loss_scale * (probability - onehot)).astype(jnp.bfloat16)


def norm_backward(grad_normed, hidden_part, rstd_part, gain_f):
    inner_sums = jnp.sum(grad_normed * gain_f * hidden_part, axis=1)
    return (
        rstd_part[:, None] * gain_f * grad_normed
        - hidden_part * (rstd_part**3)[:, None] * inner_sums[:, None] / D
    ).astype(jnp.bfloat16)


def local(hidden, gain, head, moment, second, labels):
    hidden_f = hidden.astype(jnp.float32)
    gain_f = gain.astype(jnp.float32)
    rstd = inverse_norm(hidden_f)
    normed = (hidden_f * rstd[:, None] * gain_f).astype(jnp.bfloat16)
    normed_all = lax.all_gather(normed, "dp", axis=0, tiled=True)
    all_labels = lax.all_gather(labels, "dp", axis=0, tiled=True)
    own_rows = head.shape[0]
    tensor_count = lax.axis_size("tensor")
    dp_count = lax.axis_size("dp")
    owner = lax.axis_index("dp") * tensor_count + lax.axis_index("tensor")
    vocab_ids = owner * own_rows + jnp.arange(own_rows, dtype=jnp.int32)
    logits = lax.dot_general(
        normed_all, head, (((1,), (1,)), ((), ())), preferred_element_type=jnp.float32
    )
    dlogits = softmax_grad(logits, all_labels, vocab_ids)
    grad_head = lax.dot_general(
        dlogits, normed_all, (((0,), (0,)), ((), ())), preferred_element_type=jnp.float32
    )
    share_rows = hidden.shape[0] // tensor_count
    ordered = dlogits.reshape(dp_count, tensor_count, share_rows, own_rows).transpose(1, 0, 2, 3)
    ordered = ordered.reshape(tensor_count * dp_count * share_rows, own_rows)
    tensor_sum = lax.psum_scatter(
        jnp.dot(ordered, head, preferred_element_type=jnp.float32).astype(jnp.bfloat16),
        "tensor",
        scatter_dimension=0,
        tiled=True,
    ).astype(jnp.float32)
    full_sum = lax.psum(tensor_sum, "dp")
    grad_normed = lax.dynamic_slice_in_dim(
        full_sum, lax.axis_index("dp") * share_rows, share_rows, 0
    )
    offset = lax.axis_index("tensor") * share_rows
    hidden_part = lax.dynamic_slice_in_dim(hidden_f, offset, share_rows, 0)
    rstd_part = lax.dynamic_slice_in_dim(rstd, offset, share_rows, 0)
    grad_gain = lax.psum(
        jnp.sum(grad_normed * hidden_part * rstd_part[:, None], axis=0), ("dp", "tensor")
    )
    part_grad = norm_backward(grad_normed, hidden_part, rstd_part, gain_f)
    grad_hidden = lax.all_gather(part_grad, "tensor", axis=0, tiled=True)
    row_sums = jnp.sum(grad_head * grad_head, axis=1)
    second_new = beta_two * second + (1.0 - beta_two) * row_sums / D
    first = beta_one * moment.astype(jnp.float32) + (1.0 - beta_one) * grad_head
    adam_step = first / bias_one / (jnp.sqrt(second_new / bias_two)[:, None] + adam_eps)
    head_new = (head.astype(jnp.float32) - step_size * adam_step).astype(jnp.bfloat16)
    return (grad_hidden, grad_gain, head_new, first.astype(jnp.bfloat16), second_new)


def solution(mesh):
    placed = (
        P("dp", None),
        P(),
        P(("dp", "tensor"), None),
        P(("dp", "tensor"), None),
        P(("dp", "tensor")),
        P("dp"),
    )
    return jax.shard_map(
        local,
        mesh=mesh,
        in_specs=placed,
        out_specs=(
            P("dp", None),
            P(),
            P(("dp", "tensor"), None),
            P(("dp", "tensor"), None),
            P(("dp", "tensor")),
        ),
        check_vma=False,
    )
```

profile of v0, /device:TPU:12, one launch (start us, length us, event | category | flops | bytes accessed | tf_op | source)
XLA Modules:
  0.0 299.2 jit_solution(8603135255991691037)
XLA Ops:
  7.2 0.0 copy-start
  7.2 0.0 all-gather.3.cloned.1.call-start
  7.2 0.8 convert_element_type.37
  8.0 1.0 multiply_reduce_fusion.1
  9.0 1.6 multiply_convert_fusion
  10.6 0.0 all-gather.3.cloned.1.call-update
  10.6 0.0 reduce-scatter.2.cloned.1.call-start
  10.6 1.2 dynamic-slice
  12.5 0.9 dynamic-update-slice
  13.4 12.6 %all-reduce = s32[128]{0:T(128)S(1)} all-reduce(s32[128]{0:T(128)S(1)} %dynamic-update-slice), channel_id=1, replica_groups=mesh['dp'=16,'tensor'=2] {'dp'}, use_global_device_ids=true, to_apply=%add | all-reduce | flops 128 | bytes 1024
  26.0 40.8 %all-gather.3.cloned.1.call-done = bf16[128,4096]{1,0:T(8,128)(2,1)} async-done(((bf16[8,4096]{1,0:T(8,128)(2,1)}), bf16[128,4096]{1,0:T(8,128)(2,1)}) %all-gather.3.cloned.1.call-update) | async-done | bytes 1048592 | tf_op jit(solution)/shard_map/all_gather | solution.py:45
  66.8 2.1 fusion.2
  68.9 0.0 copy-start.3
  68.9 0.0 copy-start.1
  68.9 40.0 %pmax.7 = f32[128]{0:T(128)S(1)} all-reduce(f32[128]{0:T(128)S(1)} %get-tuple-element.13), channel_id=1, replica_groups=mesh['dp'=16,'tensor'=2] {'dp','tensor'}, use_global_device_ids=true, to_apply=%region_2.0 | all-reduce | flops 128 | bytes 1024 | tf_op jit(solution)/shard_map/pmax | solution.py:25
  108.9 0.2 exponential_reduce_fusion
  109.1 40.0 %psum.21 = f32[128]{0:T(128)S(1)} all-reduce(f32[128]{0:T(128)S(1)} %exponential_multiply_fusion), channel_id=1, replica_groups=mesh['dp'=16,'tensor'=2] {'dp','tensor'}, use_global_device_ids=true, to_apply=%region_4.0 | all-reduce | flops 128 | bytes 1024 | tf_op jit(solution)/shard_map/psum | solution.py:26
  149.1 0.1 multiply_convert_fusion.1
  149.3 0.0 copy-done
  149.3 1.5 convolution_convert_fusion
  150.7 0.0 copy-start.4
  150.7 0.0 copy-start.2
  150.7 0.0 reduce-scatter.2.cloned.1.call-update
  150.8 0.0 copy-done.3
  150.8 0.1 multiply_multiply_fusion
  150.9 0.0 copy-done.1
  150.9 0.5 multiply_reduce_fusion
  151.4 0.0 copy-done.4
  151.4 0.5 sqrt_add_fusion
  152.0 0.0 copy-done.2
  152.0 2.1 fusion
  154.1 5.4 %reduce-scatter.2.cloned.1.call-done = bf16[64,4096]{1,0:T(8,128)(2,1)} async-done(((bf16[128,4096]{1,0:T(8,128)(2,1)}), bf16[64,4096]{1,0:T(8,128)(2,1)}) %reduce-scatter.2.cloned.1.call-update) | async-done | bytes 524304 | tf_op jit(solution)/shard_map/reduce_scatter | solution.py:62
  159.5 81.5 %all-reduce.2 = f32[64,4096]{1,0:T(8,128)S(1)} all-reduce(bf16[64,4096]{1,0:T(8,128)(2,1)} %reduce-scatter.2.cloned.1.call-done), channel_id=1, replica_groups=mesh['dp'=16,'tensor'=2] {'dp'}, use_global_device_ids=true, to_apply=%region_6.0 | all-reduce | flops 262144 | bytes 1572864 | tf_op jit(solution)/shard_map/psum | solution.py:68
  241.0 0.2 multiply_reduce_fusion.2
  241.2 0.1 fusion.1
  241.3 1.9 all-gather
  243.1 0.7 reshape.41
  243.8 48.6 %psum.23 = f32[4096]{0:T(1024)} all-reduce(f32[4096]{0:T(1024)S(1)} %get-tuple-element.5), channel_id=1, replica_groups=mesh['dp'=16,'tensor'=2] {'dp','tensor'}, use_global_device_ids=true, to_apply=%region_9.0 | all-reduce | flops 4096 | bytes 32768 | tf_op jit(solution)/shard_map/psum | solution.py:75
  (6 shorter events, 0.0 us)
Async XLA Ops:
  7.2 142.1 %copy-start = (bf16[128,4096]{1,0:T(8,128)(2,1)S(1)}, bf16[128,4096]{1,0:T(8,128)(2,1)}, u32[]{:S(2)}) copy-start(bf16[128,4096]{1,0:T(8,128)(2,1)} %param.8) | copy-start | bytes 3145732
  7.2 59.6 %all-gather.3.cloned.1.call-start = ((), (), s32[]{:S(2)}) async-start(), calls=%async_computation.1 | async-start | bytes 1114112 | tf_op jit(solution)/shard_map/all_gather | solution.py:45
  10.6 148.9 %reduce-scatter.2.cloned.1.call-start = ((), (), s32[]{:S(2)}) async-start(), calls=%async_computation.2 | async-start | bytes 1572864 | tf_op jit(solution)/shard_map/reduce_scatter | solution.py:62
  68.9 81.9 %copy-start.3 = (bf16[8,4096]{1,0:T(8,128)(2,1)S(1)}, bf16[8,4096]{1,0:T(8,128)(2,1)}, u32[]{:S(2)}) copy-start(bf16[8,4096]{1,0:T(8,128)(2,1)} %param.6) | copy-start | bytes 196612
  68.9 82.0 %copy-start.1 = (bf16[128,4096]{1,0:T(8,128)(2,1)S(1)}, bf16[128,4096]{1,0:T(8,128)(2,1)}, u32[]{:S(2)}) copy-start(bf16[128,4096]{1,0:T(8,128)(2,1)} %all-gather.3.cloned.1.call-done) | copy-start | bytes 3145732
  150.7 0.7 copy-start.4
  150.7 1.2 copy-start.2
Sparse Core Ops, SparseCore 0:
  11.3 55.4 all-gather.2
  150.9 8.5 reduce-scatter.1
where the time goes:
time: 300 us; the launch traced here: 299 us
  blocking collectives  225 us (75%)
  waiting for transfers between devices  46.2 us (15%)
  between operations  14.8 us (5%)
  other arithmetic  6.64 us (2%)
  matrix products  4.05 us (1%)
    psum x1, blocking collectives, local(): full_sum = lax.psum(tensor_sum, 'dp')  81.5 us
    psum x1, blocking collectives, local(): lax.psum(jnp.sum(grad_normed * hidden_part * rstd_part[:, None], axis=0),...  48.6 us
    all_gather x1, waiting for transfers between devices, local(): normed_all = lax.all_gather(normed, 'dp', axis=0, tiled=True)  40.8 us
    pmax x1, blocking collectives, softmax_grad(): global_max = lax.pmax(local_max, ('dp', 'tensor'))  40 us
    psum x1, blocking collectives, softmax_grad(): lax.psum(local_sum * jnp.exp(local_max - global_max), ('dp', 'tensor'))  40 us
    unnamed x1, blocking collectives  12.6 us
  transfers between devices with their start and end apart: 2, of which 2 were waited for; matrix products, arithmetic and copies ran while one was open for 2% of the time, Pallas kernels for 0%

commit v1 on v0

--- a/solution.py
+++ b/solution.py
@@ -65,7 +65,9 @@
         scatter_dimension=0,
         tiled=True,
     ).astype(jnp.float32)
-    full_sum = lax.psum(tensor_sum, "dp")
+    full_sum = tensor_sum
+    for hop in (1, 2, 4, 8):
+        full_sum = full_sum + lax.ppermute(full_sum, "dp", [(dev, dev ^ hop) for dev in range(16)])
     grad_normed = lax.dynamic_slice_in_dim(
         full_sum, lax.axis_index("dp") * share_rows, share_rows, 0
     )

time: 300 us -> 335 us (1.12)
  waiting for transfers between devices: 46.2 us -> 160 us
  blocking collectives: 225 us -> 137 us
  starting transfers between devices: 0.08 us -> 5.25 us
  other arithmetic: 6.64 us -> 10.3 us
    ppermute x0 -> x4, waiting for transfers between devices: none -> 111 us  [local(): lax.ppermute(full_sum, 'dp', [(dev, dev ^ hop) for dev in range(16)])]
    psum x1 -> x0, blocking collectives: 81.5 us -> none  [local(): full_sum = lax.psum(tensor_sum, 'dp')]
    psum x1, blocking collectives: 48.6 us -> 42.6 us  [local(): lax.psum(jnp.sum(grad_normed * hidden_part * rstd_part[:, None], axis=0),...]
    ppermute x0 -> x4, starting transfers between devices: none -> 5.17 us  [local(): lax.ppermute(full_sum, 'dp', [(dev, dev ^ hop) for dev in range(16)])]
  transfers between devices with their start and end apart: 2 -> 6, of which waited for: 2 -> 6; matrix products, arithmetic and copies ran while one was open for 2% -> 2% of each run, Pallas kernels for 0% -> 0%
where the time goes in v1:
time: 335 us; the launch traced here: 334 us
  waiting for transfers between devices  160 us (48%)
  blocking collectives  137 us (41%)
  between operations  14.8 us (4%)
  other arithmetic  10.3 us (3%)
  starting transfers between devices  5.25 us (2%)
  matrix products  3.99 us (1%)
    ppermute x4, waiting for transfers between devices, local(): lax.ppermute(full_sum, 'dp', [(dev, dev ^ hop) for dev in range(16)])  111 us
    psum x1, blocking collectives, local(): lax.psum(jnp.sum(grad_normed * hidden_part * rstd_part[:, None], axis=0),...  42.6 us
    all_gather x1, waiting for transfers between devices, local(): normed_all = lax.all_gather(normed, 'dp', axis=0, tiled=True)  40.8 us
    pmax x1, blocking collectives, softmax_grad(): global_max = lax.pmax(local_max, ('dp', 'tensor'))  40 us
    psum x1, blocking collectives, softmax_grad(): lax.psum(local_sum * jnp.exp(local_max - global_max), ('dp', 'tensor'))  40 us
    unnamed x1, blocking collectives  12.6 us
    reduce_scatter x1, waiting for transfers between devices, local(): lax.psum_scatter(jnp.dot(ordered, head, preferred_element_type=jnp.float3...  8.69 us
  transfers between devices with their start and end apart: 6, of which 6 were waited for; matrix products, arithmetic and copies ran while one was open for 2% of the time, Pallas kernels for 0%

profile of v1, /device:TPU:12, one launch (start us, length us, event | category | flops | bytes accessed | tf_op | source)
XLA Modules:
  0.0 334.5 jit_solution(3166009098841074514)
XLA Ops:
  7.2 0.0 copy-start
  7.2 0.0 all-gather.3.cloned.1.call-start
  7.2 0.8 convert_element_type.37
  8.0 1.0 multiply_reduce_fusion.1
  9.0 1.6 multiply_convert_fusion
  10.6 0.0 all-gather.3.cloned.1.call-update
  10.6 0.0 reduce-scatter.2.cloned.1.call-start
  10.6 1.2 dynamic-slice
  12.5 0.9 dynamic-update-slice
  13.4 12.6 %all-reduce = s32[128]{0:T(128)S(1)} all-reduce(s32[128]{0:T(128)S(1)} %dynamic-update-slice), channel_id=1, replica_groups=mesh['dp'=16,'tensor'=2] {'dp'}, use_global_device_ids=true, to_apply=%add | all-reduce | flops 128 | bytes 1024
  26.0 40.8 %all-gather.3.cloned.1.call-done = bf16[128,4096]{1,0:T(8,128)(2,1)} async-done(((bf16[8,4096]{1,0:T(8,128)(2,1)}), bf16[128,4096]{1,0:T(8,128)(2,1)}) %all-gather.3.cloned.1.call-update) | async-done | bytes 1048592 | tf_op jit(solution)/shard_map/all_gather | solution.py:45
  66.8 2.1 fusion.2
  68.9 40.0 %pmax.7 = f32[128]{0:T(128)S(1)} all-reduce(f32[128]{0:T(128)S(1)} %get-tuple-element.14), channel_id=1, replica_groups=mesh['dp'=16,'tensor'=2] {'dp','tensor'}, use_global_device_ids=true, to_apply=%region_2.0 | all-reduce | flops 128 | bytes 1024 | tf_op jit(solution)/shard_map/pmax | solution.py:25
  108.9 0.2 exponential_reduce_fusion
  109.1 40.0 %psum.14 = f32[128]{0:T(128)S(1)} all-reduce(f32[128]{0:T(128)S(1)} %exponential_multiply_fusion), channel_id=1, replica_groups=mesh['dp'=16,'tensor'=2] {'dp','tensor'}, use_global_device_ids=true, to_apply=%region_4.0 | all-reduce | flops 128 | bytes 1024 | tf_op jit(solution)/shard_map/psum | solution.py:26
  149.1 0.1 multiply_convert_fusion.1
  149.3 0.0 copy-done
  149.3 1.4 convolution_convert_fusion
  150.7 0.0 reduce-scatter.2.cloned.1.call-update
  150.7 8.7 %reduce-scatter.2.cloned.1.call-done = bf16[64,4096]{1,0:T(8,128)(2,1)} async-done(((bf16[128,4096]{1,0:T(8,128)(2,1)}), bf16[64,4096]{1,0:T(8,128)(2,1)}) %reduce-scatter.2.cloned.1.call-update) | async-done | bytes 524304 | tf_op jit(solution)/shard_map/reduce_scatter | solution.py:62
  159.4 1.1 convert_element_type.42
  160.5 1.5 collective-permute-start
  162.0 23.9 %collective-permute-done = f32[64,4096]{1,0:T(8,128)S(1)} collective-permute-done((f32[64,4096]{1,0:T(8,128)S(1)}, f32[64,4096]{1,0:T(8,128)S(1)}, u32[]{:S(2)}, u32[]{:S(2)}) %collective-permute-start) | collective-permute-done | bytes 1048608 | tf_op jit(solution)/shard_map/ppermute | solution.py:70
  186.0 1.1 convert_add_fusion
  187.1 0.0 copy-start.3
  187.1 0.0 copy-start.1
  187.1 0.6 collective-permute-start.1
  187.7 24.1 %collective-permute-done.1 = f32[64,4096]{1,0:T(8,128)S(1)} collective-permute-done((f32[64,4096]{1,0:T(8,128)S(1)}, f32[64,4096]{1,0:T(8,128)S(1)}, u32[]{:S(2)}, u32[]{:S(2)}) %collective-permute-start.1) | collective-permute-done | bytes 1048608 | tf_op jit(solution)/shard_map/ppermute | solution.py:70
  211.8 0.1 add.64
  211.9 0.0 copy-start.4
  211.9 0.6 collective-permute-start.2
  212.5 0.0 copy-done.3
  212.5 0.1 multiply_multiply_fusion
  212.6 0.0 copy-done.1
  212.6 0.5 multiply_reduce_fusion
  213.1 0.0 copy-start.2
  213.1 0.5 sqrt_add_fusion
  213.6 22.1 %collective-permute-done.2 = f32[64,4096]{1,0:T(8,128)} collective-permute-done((f32[64,4096]{1,0:T(8,128)S(1)}, f32[64,4096]{1,0:T(8,128)}, u32[]{:S(2)}, u32[]{:S(2)}) %collective-permute-start.2) | collective-permute-done | bytes 1048608 | tf_op jit(solution)/shard_map/ppermute | solution.py:70
  235.8 1.3 add.65
  237.1 2.5 collective-permute-start.3
  239.6 0.0 copy-done.2
  239.6 2.1 fusion
  241.6 40.5 %collective-permute-done.3 = f32[64,4096]{1,0:T(8,128)S(1)} collective-permute-done((f32[64,4096]{1,0:T(8,128)S(1)}, f32[64,4096]{1,0:T(8,128)S(1)}, u32[]{:S(2)}, u32[]{:S(2)}) %collective-permute-start.3) | collective-permute-done | bytes 1048608 | tf_op jit(solution)/shard_map/ppermute | solution.py:70
  282.2 0.2 multiply_reduce_fusion.2
  282.4 0.1 fusion.1
  282.5 1.9 all-gather
  284.3 0.7 reshape.41
  285.0 42.6 %psum.15 = f32[4096]{0:T(1024)} all-reduce(f32[4096]{0:T(1024)S(1)} %get-tuple-element.5), channel_id=1, replica_groups=mesh['dp'=16,'tensor'=2] {'dp','tensor'}, use_global_device_ids=true, to_apply=%region_8.0 | all-reduce | flops 4096 | bytes 32768 | tf_op jit(solution)/shard_map/psum | solution.py:77
  (7 shorter events, 0.0 us)
Async XLA Ops:
  7.2 142.1 %copy-start = (bf16[128,4096]{1,0:T(8,128)(2,1)S(1)}, bf16[128,4096]{1,0:T(8,128)(2,1)}, u32[]{:S(2)}) copy-start(bf16[128,4096]{1,0:T(8,128)(2,1)} %param.8) | copy-start | bytes 3145732
  7.2 59.6 %all-gather.3.cloned.1.call-start = ((), (), s32[]{:S(2)}) async-start(), calls=%async_computation.1 | async-start | bytes 1114112 | tf_op jit(solution)/shard_map/all_gather | solution.py:45
  10.6 148.8 %reduce-scatter.2.cloned.1.call-start = ((), (), s32[]{:S(2)}) async-start(), calls=%async_computation.2 | async-start | bytes 1572864 | tf_op jit(solution)/shard_map/reduce_scatter | solution.py:62
  160.5 25.5 %collective-permute-start = (f32[64,4096]{1,0:T(8,128)S(1)}, f32[64,4096]{1,0:T(8,128)S(1)}, u32[]{:S(2)}, u32[]{:S(2)}) collective-permute-start(f32[64,4096]{1,0:T(8,128)S(1)} %convert_element_type.42), channel_id=1, source_target_pairs={{0,2},{2,0},{4,6},{6,4},{8,10},{10,8},{12,14},{14,12},{16,18},{18,... | collective-permute-start | bytes 3145736 | tf_op jit(solution)/shard_map/ppermute | solution.py:70
  187.1 25.4 %copy-start.3 = (bf16[8,4096]{1,0:T(8,128)(2,1)S(1)}, bf16[8,4096]{1,0:T(8,128)(2,1)}, u32[]{:S(2)}) copy-start(bf16[8,4096]{1,0:T(8,128)(2,1)} %param.6) | copy-start | bytes 196612
  187.1 25.5 %copy-start.1 = (bf16[128,4096]{1,0:T(8,128)(2,1)S(1)}, bf16[128,4096]{1,0:T(8,128)(2,1)}, u32[]{:S(2)}) copy-start(bf16[128,4096]{1,0:T(8,128)(2,1)} %all-gather.3.cloned.1.call-done) | copy-start | bytes 3145732
  187.1 24.7 %collective-permute-start.1 = (f32[64,4096]{1,0:T(8,128)S(1)}, f32[64,4096]{1,0:T(8,128)S(1)}, u32[]{:S(2)}, u32[]{:S(2)}) collective-permute-start(f32[64,4096]{1,0:T(8,128)S(1)} %convert_add_fusion), channel_id=1, source_target_pairs={{0,4},{2,6},{4,0},{6,2},{8,12},{10,14},{12,8},{14,10},{16,20},{18,... | collective-permute-start | bytes 3145736 | tf_op jit(solution)/shard_map/ppermute | solution.py:70
  211.9 1.2 copy-start.4
  211.9 23.9 %collective-permute-start.2 = (f32[64,4096]{1,0:T(8,128)S(1)}, f32[64,4096]{1,0:T(8,128)}, u32[]{:S(2)}, u32[]{:S(2)}) collective-permute-start(f32[64,4096]{1,0:T(8,128)S(1)} %add.64), channel_id=1, source_target_pairs={{0,8},{2,10},{4,12},{6,14},{8,0},{10,2},{12,4},{14,6},{16,24},{18,... | collective-permute-start | bytes 3145736 | tf_op jit(solution)/shard_map/ppermute | solution.py:70
  213.1 26.5 %copy-start.2 = (bf16[128,4096]{1,0:T(8,128)(2,1)S(1)}, bf16[128,4096]{1,0:T(8,128)(2,1)}, u32[]{:S(2)}) copy-start(bf16[128,4096]{1,0:T(8,128)(2,1)} %param.9) | copy-start | bytes 3145732
  237.1 45.1 %collective-permute-start.3 = (f32[64,4096]{1,0:T(8,128)S(1)}, f32[64,4096]{1,0:T(8,128)S(1)}, u32[]{:S(2)}, u32[]{:S(2)}) collective-permute-start(f32[64,4096]{1,0:T(8,128)S(1)} %add.65), channel_id=1, source_target_pairs={{0,16},{2,18},{4,20},{6,22},{8,24},{10,26},{12,28},{14,30},{16,0},... | collective-permute-start | bytes 3145736 | tf_op jit(solution)/shard_map/ppermute | solution.py:70
Sparse Core Ops, SparseCore 0:
  11.3 55.4 all-gather.2
  150.8 8.5 reduce-scatter.1
